TPU v7x, 256 devices: a whole 4x4x8 slice. The times are simulated.
256 devices in a mesh: dp: 8 (over y, core), seq: 32 (over x, z).
Axes of the slice: x: 4, y: 4, z: 8, core: 2. Of those that a mesh axis runs over, the one named last changes fastest.
Arguments:
- token_ids: int32 [8, 4096], P('dp', 'seq'), may hold values from 0 to 255
- cotangent: bfloat16 [8, 4096, 768], P('dp', 'seq'), may hold values from -6 to 6
- table: bfloat16 [256, 768], replicated, may hold values from -12 to 12
- w_query: bfloat16 [768, 768], replicated, may hold values from -2 to 2
- w_key: bfloat16 [768, 768], replicated, may hold values from -2 to 2
- w_value: bfloat16 [768, 768], replicated, may hold values from -0.21875 to 0.21875
- w_out: bfloat16 [768, 768], replicated, may hold values from -0.21875 to 0.21875
- window: int32 [12], replicated, may hold values from 64 to 512, as said below
Outputs:
- grad_input: bfloat16 [8, 4096, 768], P('dp', 'seq')
- weight_grads: float32 [3072, 768], P('seq')
Inputs may be any that keep to these rules, and one draw needn't show every extreme that they name: Some head's window is exactly 512.
All inputs are finite; a program needn't handle non-finite values.
Results may differ from a plain program's by a relative error of at most 0.025.
Values may be sent and summed in bfloat16 or wider, within the bound.
A program may use at most 128 MiB of HBM per device.

v0:
```python
import jax
import jax.numpy as jnp
from jax import lax
from jax.sharding import PartitionSpec as P

HEADS = 12
HEAD_DIM = 64
WINDOW = 512
EPSILON = 1e-05


def shifted(block, axis, distance):
    devices = range(lax.axis_size(axis))
    route = [(i - distance, i) for i in devices if i - distance in devices]
    return lax.ppermute(block, axis, route)


def rotate(values, positions):
    row_count = values.shape[0]
    shaped = values.reshape(row_count, -1, HEAD_DIM)
    middle = HEAD_DIM // 2
    frequency = 10000.0 ** (-2.0 * jnp.arange(middle, dtype=jnp.float32) / HEAD_DIM)
    angles = positions.astype(jnp.float32)[:, None] * frequency[None, :]
    cosine = jnp.cos(angles)[:, None, :]
    sine_part = jnp.sin(angles)[:, None, :]
    former = shaped[..., :middle]
    latter = shaped[..., middle:]
    turned = jnp.concatenate(
        [former * cosine - latter * sine_part, latter * cosine + former * sine_part], axis=-1
    )
    return turned.reshape(row_count, -1)


def unrotate(values, positions):
    row_count = values.shape[0]
    shaped = values.reshape(row_count, -1, HEAD_DIM)
    middle = HEAD_DIM // 2
    frequency = 10000.0 ** (-2.0 * jnp.arange(middle, dtype=jnp.float32) / HEAD_DIM)
    angles = positions.astype(jnp.float32)[:, None] * frequency[None, :]
    cosine = jnp.cos(angles)[:, None, :]
    sine_part = jnp.sin(angles)[:, None, :]
    former = shaped[..., :middle]
    latter = shaped[..., middle:]
    turned = jnp.concatenate(
        [former * cosine + latter * sine_part, latter * cosine - former * sine_part], axis=-1
    )
    return turned.reshape(row_count, -1)


def tdot(left, right):
    return lax.dot_general(
        left, right, (((0,), (0,)), ((), ())), preferred_element_type=jnp.float32
    )


def ndot(left, right):
    return lax.dot_general(
        left, right, (((1,), (1,)), ((), ())), preferred_element_type=jnp.float32
    )


def embed_rows(byte_ids, table):
    onehot = (byte_ids[:, None] == jnp.arange(table.shape[0], dtype=jnp.int32)[None, :]).astype(
        jnp.bfloat16
    )
    return jnp.dot(onehot, table, preferred_element_type=jnp.float32).astype(jnp.bfloat16)


def normalize(embedded):
    widened = embedded.astype(jnp.float32)
    inv_rms = lax.rsqrt(jnp.mean(widened * widened, axis=1, keepdims=True) + EPSILON)
    return (widened, inv_rms, (widened * inv_rms).astype(jnp.bfloat16))


def keys_values(normed, positions, w_key, w_value):
    key_rows = rotate(jnp.dot(normed, w_key, preferred_element_type=jnp.float32), positions).astype(
        jnp.bfloat16
    )
    value_rows = jnp.dot(normed, w_value, preferred_element_type=jnp.float32).astype(jnp.bfloat16)
    return (key_rows, value_rows)


def head_group(
    query_heads, key_heads, value_heads, grad_heads, group_window, own_pos, key_pos, score_scale
):
    distance = own_pos[:, None] - key_pos[None, :]
    allowed = (
        (distance[None] >= 0)
        & (distance[None] < group_window[:, None, None])
        & (key_pos[None, None, :] >= 0)
    )
    scores = (
        jnp.einsum("qhd,khd->hqk", query_heads, key_heads, preferred_element_type=jnp.float32)
        * score_scale
    )
    masked = jnp.where(allowed, scores, -1e30)
    row_max = jnp.max(masked, axis=-1, keepdims=True)
    weights = jnp.where(allowed, jnp.exp(masked - row_max), 0.0)
    probs = weights / jnp.sum(weights, axis=-1, keepdims=True)
    probs_b = probs.astype(jnp.bfloat16)
    attended = jnp.einsum(
        "hqk,khd->qhd", probs_b, value_heads, preferred_element_type=jnp.float32
    ).astype(jnp.bfloat16)
    grad_probs = jnp.einsum(
        "qhd,khd->hqk", grad_heads, value_heads, preferred_element_type=jnp.float32
    )
    row_term = jnp.sum(probs * grad_probs, axis=-1, keepdims=True)
    grad_scores = (probs * (grad_probs - row_term) * score_scale).astype(jnp.bfloat16)
    grad_query = jnp.einsum(
        "hqk,khd->qhd", grad_scores, key_heads, preferred_element_type=jnp.float32
    )
    grad_key = jnp.einsum(
        "hqk,qhd->khd", grad_scores, query_heads, preferred_element_type=jnp.float32
    )
    grad_value = jnp.einsum("hqk,qhd->khd", probs_b, grad_heads, preferred_element_type=jnp.float32)
    return (attended, grad_query, grad_key, grad_value)


def on_device(token_ids, cotangent, table, w_query, w_key, w_value, w_out, window):
    local_ids = token_ids[0]
    grad_out = cotangent[0]
    length = local_ids.shape[0]
    features = table.shape[1]
    tail_rows = min(length, WINDOW)
    reach_devs = -(-WINDOW // length)
    halo_rows = reach_devs * tail_rows
    offset = lax.axis_index("seq") * length
    own_pos = offset + jnp.arange(length, dtype=jnp.int32)
    halo_pos = offset - halo_rows + jnp.arange(halo_rows, dtype=jnp.int32)
    score_scale = HEAD_DIM ** (-0.5)
    embedded = embed_rows(local_ids, table)
    widened, inv_rms, normed = normalize(embedded)
    query = rotate(jnp.dot(normed, w_query, preferred_element_type=jnp.float32), own_pos).astype(
        jnp.bfloat16
    )
    key_own, value_own = keys_values(normed, own_pos, w_key, w_value)
    key_pieces = []
    value_pieces = []
    for hop_index in range(reach_devs):
        far_keys, far_values = shifted((key_own, value_own), "seq", hop_index + 1)
        key_pieces.insert(0, far_keys)
        value_pieces.insert(0, far_values)
    key_halo = jnp.concatenate(key_pieces, axis=0)
    value_halo = jnp.concatenate(value_pieces, axis=0)
    span_rows = halo_rows + length
    key_all = jnp.concatenate([key_halo, key_own], axis=0)
    value_all = jnp.concatenate([value_halo, value_own], axis=0)
    key_pos = jnp.concatenate([halo_pos, own_pos], axis=0)
    query_heads = query.reshape(length, HEADS, HEAD_DIM)
    key_heads = key_all.reshape(span_rows, HEADS, HEAD_DIM)
    value_heads = value_all.reshape(span_rows, HEADS, HEAD_DIM)
    grad_att = ndot(grad_out, w_out).astype(jnp.bfloat16)
    grad_heads = grad_att.reshape(length, HEADS, HEAD_DIM)
    group_size = 4
    attended_parts = []
    query_parts = []
    key_parts = []
    value_parts = []
    for group_index in range(HEADS // group_size):
        lower = group_index * group_size
        upper = lower + group_size
        outputs = head_group(
            query_heads[:, lower:upper],
            key_heads[:, lower:upper],
            value_heads[:, lower:upper],
            grad_heads[:, lower:upper],
            window[lower:upper],
            own_pos,
            key_pos,
            score_scale,
        )
        attended_parts.append(outputs[0])
        query_parts.append(outputs[1])
        key_parts.append(outputs[2])
        value_parts.append(outputs[3])
    attended = jnp.concatenate(attended_parts, axis=1).reshape(length, features)
    grad_query = jnp.concatenate(query_parts, axis=1).reshape(length, features)
    grad_key = jnp.concatenate(key_parts, axis=1).reshape(span_rows, features)
    grad_value = jnp.concatenate(value_parts, axis=1).reshape(span_rows, features)
    tail_keys = grad_key[:halo_rows].reshape(reach_devs, tail_rows, features)
    tail_values = grad_value[:halo_rows].reshape(reach_devs, tail_rows, features)
    back_keys = jnp.zeros((tail_rows, features), jnp.float32)
    back_values = jnp.zeros((tail_rows, features), jnp.float32)
    for hop_index in range(reach_devs):
        got_keys, got_values = shifted(
            (tail_keys[reach_devs - 1 - hop_index], tail_values[reach_devs - 1 - hop_index]),
            "seq",
            -(hop_index + 1),
        )
        back_keys = back_keys + got_keys
        back_values = back_values + got_values
    own_keys = grad_key[halo_rows:]
    own_values = grad_value[halo_rows:]
    own_keys = jnp.concatenate([own_keys[: length - tail_rows], own_keys + back_keys], axis=0)
    own_values = jnp.concatenate(
        [own_values[: length - tail_rows], own_values + back_values], axis=0
    )
    grad_q_lin = unrotate(grad_query, own_pos).astype(jnp.bfloat16)
    grad_k_lin = unrotate(own_keys, own_pos).astype(jnp.bfloat16)
    grad_v_lin = own_values.astype(jnp.bfloat16)
    grad_normed = ndot(grad_q_lin, w_query) + ndot(grad_k_lin, w_key) + ndot(grad_v_lin, w_value)
    scaled = widened * inv_rms
    grad_input = (
        inv_rms * (grad_normed - scaled * jnp.mean(grad_normed * scaled, axis=1, keepdims=True))
    ).astype(jnp.bfloat16)
    term = jnp.concatenate(
        [
            tdot(normed, grad_q_lin),
            tdot(normed, grad_k_lin),
            tdot(normed, grad_v_lin),
            tdot(attended, grad_out),
        ],
        axis=0,
    )
    shares = lax.psum_scatter(term.astype(jnp.bfloat16), "seq", scatter_dimension=0, tiled=True)
    weight_grads = lax.psum(shares, "dp").astype(jnp.float32)
    return (grad_input[None], weight_grads)


def solution(mesh):
    return jax.shard_map(
        on_device,
        mesh=mesh,
        in_specs=(P("dp", "seq"), P("dp", "seq", None), P(), P(), P(), P(), P(), P()),
        out_specs=(P("dp", "seq", None), P("seq", None)),
        check_vma=False,
    )
```

profile of v0, /device:TPU:2, one launch (start us, length us, event | category | flops | bytes accessed | tf_op | source)
XLA Modules:
  0.0 592.0 jit_solution(5560135934124274321)
XLA Ops:
  10.5 3.8 collective-permute-start.7
  14.3 5.2 collective-permute-start.6
  19.5 5.9 %collective-permute-start.5 = (bf16[128,768]{1,0:T(8,128)(2,1)}, bf16[128,768]{1,0:T(8,128)(2,1)}, u32[]{:S(2)}, u32[]{:S(2)}) collective-permute-start(bf16[128,768]{1,0:T(8,128)(2,1)} %convolution_convert_fusion.4), channel_id=1, source_target_pairs={{0,3},{1,4},{2,5},{3,6},{4,7},{5,8},{6,9},{7,10},{8,11},{9,12},{10... | collective-permute-start | bytes 589832 | tf_op jit(solution)/shard_map/ppermute | solution.py:15
  25.4 3.4 collective-permute-start.4
  32.4 3.8 collective-permute-start.3
  37.7 2.5 convolution_convert_fusion.5
  44.0 6.0 %collective-permute-done.4 = bf16[128,768]{1,0:T(8,128)(2,1)} collective-permute-done((bf16[128,768]{1,0:T(8,128)(2,1)}, bf16[128,768]{1,0:T(8,128)(2,1)}, u32[]{:S(2)}, u32[]{:S(2)}) %collective-permute-start.4) | collective-permute-done | bytes 196640 | tf_op jit(solution)/shard_map/ppermute | solution.py:15
  50.0 9.0 %collective-permute-start.2 = (bf16[128,768]{0,1:T(8,128)(2,1)}, bf16[128,768]{0,1:T(8,128)(2,1)}, u32[]{:S(2)}, u32[]{:S(2)}) collective-permute-start(bf16[128,768]{0,1:T(8,128)(2,1)} %bitcast.2), channel_id=1, source_target_pairs={{0,2},{1,3},{2,4},{3,5},{4,6},{5,7},{6,8},{7,9},{8,10},{9,11},{10,... | collective-permute-start | bytes 589832 | tf_op jit(solution)/shard_map/ppermute | solution.py:15
  64.2 5.2 collective-permute-start
  76.5 9.6 %collective-permute-done = bf16[128,768]{0,1:T(8,128)(2,1)} collective-permute-done((bf16[128,768]{0,1:T(8,128)(2,1)}, bf16[128,768]{0,1:T(8,128)(2,1)}, u32[]{:S(2)}, u32[]{:S(2)}) %collective-permute-start) | collective-permute-done | bytes 196640 | tf_op jit(solution)/shard_map/ppermute | solution.py:15
  100.7 6.0 %fusion.55 = f32[128,4,64]{0,2,1:T(8,128)} fusion(bf16[640,12,64]{0,2,1:T(8,128)(2,1)} %bitcast.121, f32[4,128,640]{2,1,0:T(8,128)} %fusion.68, f32[4,128,640]{2,1,0:T(8,128)} %copy-done.8, f32[4,128]{1,0:T(4,128)} %copy-done.43), kind=kOutput, calls=%fused_computation.66 | convolution fusion | flops 44237952 | bytes 3737600 | tf_op jit(solution)/shard_map/hqk,khd->qhd/dot_general | solution.py:109
  106.7 6.1 %convolution_bitcast_fusion.3 = f32[640,4,64]{0,2,1:T(8,128)} fusion(f32[4,128,640]{2,1,0:T(8,128)} %fusion.68, bf16[128,12,32]{0,2,1:T(8,128)(2,1)} %get-tuple-element.17, bf16[128,12,32]{0,2,1:T(8,128)(2,1)} %get-tuple-element.16, f32[4,128,640]{2,1,0:T(8,128)} %copy-done.8, f32[4,128]{1,0:T(4,128)} %copy-done.43), kind=kOutput, calls=%fused_computation.46 | convolution fusion | flops 44631168 | bytes 3475456 | tf_op jit(solution)/shard_map/hqk,qhd->khd/dot_general | solution.py:112
  112.8 2.6 convolution_bitcast_fusion
  119.8 5.8 fusion.52
  125.6 6.0 %convolution_bitcast_fusion.4 = f32[640,4,64]{0,2,1:T(8,128)} fusion(f32[4,128,640]{2,1,0:T(8,128)} %fusion.71, bf16[128,12,32]{0,2,1:T(8,128)(2,1)} %get-tuple-element.17, bf16[128,12,32]{0,2,1:T(8,128)(2,1)} %get-tuple-element.16, f32[4,128,640]{2,1,0:T(8,128)} %copy-done.9, f32[4,128]{1,0:T(4,128)} %copy-done.44), kind=kOutput, calls=%fused_computation.47 | convolution fusion | flops 44631168 | bytes 3475456 | tf_op jit(solution)/shard_map/hqk,qhd->khd/dot_general | solution.py:112
  131.6 2.6 convolution_bitcast_fusion.1
  138.0 5.2 fusion.49
  143.2 5.9 convolution_bitcast_fusion.5
  153.1 3.6 collective-permute-start.15
  156.7 4.5 collective-permute-start.13
  167.6 10.3 %collective-permute-done.15 = f32[128,768]{0,1:T(8,128)S(1)} collective-permute-done((f32[128,768]{0,1:T(8,128)S(1)}, f32[128,768]{0,1:T(8,128)S(1)}, u32[]{:S(2)}, u32[]{:S(2)}) %collective-permute-start.15) | collective-permute-done | bytes 393248 | tf_op jit(solution)/shard_map/ppermute | solution.py:15
  177.9 7.2 %collective-permute-start.9 = (f32[128,768]{0,1:T(8,128)S(1)}, f32[128,768]{0,1:T(8,128)S(1)}, u32[]{:S(2)}, u32[]{:S(2)}) collective-permute-start(f32[128,768]{0,1:T(8,128)S(1)} %bitcast.114), channel_id=1, source_target_pairs={{2,0},{3,1},{4,2},{5,3},{6,4},{7,5},{8,6},{9,7},{10,8},{11,9},{12,... | collective-permute-start | bytes 1179656 | tf_op jit(solution)/shard_map/ppermute | solution.py:15
  185.1 13.0 %collective-permute-done.13 = f32[128,768]{0,1:T(8,128)S(1)} collective-permute-done((f32[128,768]{0,1:T(8,128)S(1)}, f32[128,768]{0,1:T(8,128)S(1)}, u32[]{:S(2)}, u32[]{:S(2)}) %collective-permute-start.13) | collective-permute-done | bytes 393248 | tf_op jit(solution)/shard_map/ppermute | solution.py:15
  198.1 10.3 %collective-permute-start.10 = (f32[128,768]{0,1:T(8,128)S(1)}, f32[128,768]{0,1:T(8,128)S(1)}, u32[]{:S(2)}, u32[]{:S(2)}) collective-permute-start(f32[128,768]{0,1:T(8,128)S(1)} %bitcast.113), channel_id=1, source_target_pairs={{3,0},{4,1},{5,2},{6,3},{7,4},{8,5},{9,6},{10,7},{11,8},{12,9},{13... | collective-permute-start | bytes 1179656 | tf_op jit(solution)/shard_map/ppermute | solution.py:15
  208.4 9.7 %collective-permute-done.14 = f32[128,768]{0,1:T(8,128)S(1)} collective-permute-done((f32[128,768]{0,1:T(8,128)S(1)}, f32[128,768]{0,1:T(8,128)S(1)}, u32[]{:S(2)}, u32[]{:S(2)}) %collective-permute-start.14) | collective-permute-done | bytes 393248 | tf_op jit(solution)/shard_map/ppermute | solution.py:15
  220.0 28.5 %collective-permute-done.12 = f32[128,768]{0,1:T(8,128)S(1)} collective-permute-done((f32[128,768]{0,1:T(8,128)S(1)}, f32[128,768]{0,1:T(8,128)S(1)}, u32[]{:S(2)}, u32[]{:S(2)}) %collective-permute-start.12) | collective-permute-done | bytes 393248 | tf_op jit(solution)/shard_map/ppermute | solution.py:15
  249.3 17.1 %collective-permute-done.9 = f32[128,768]{0,1:T(8,128)S(1)} collective-permute-done((f32[128,768]{0,1:T(8,128)S(1)}, f32[128,768]{0,1:T(8,128)S(1)}, u32[]{:S(2)}, u32[]{:S(2)}) %collective-permute-start.9) | collective-permute-done | bytes 393248 | tf_op jit(solution)/shard_map/ppermute | solution.py:15
  266.3 18.8 %collective-permute-done.10 = f32[128,768]{0,1:T(8,128)S(1)} collective-permute-done((f32[128,768]{0,1:T(8,128)S(1)}, f32[128,768]{0,1:T(8,128)S(1)}, u32[]{:S(2)}, u32[]{:S(2)}) %collective-permute-start.10) | collective-permute-done | bytes 393248 | tf_op jit(solution)/shard_map/ppermute | solution.py:15
  285.1 8.3 %collective-permute-done.8 = f32[128,768]{0,1:T(8,128)S(1)} collective-permute-done((f32[128,768]{0,1:T(8,128)S(1)}, f32[128,768]{0,1:T(8,128)S(1)}, u32[]{:S(2)}, u32[]{:S(2)}) %collective-permute-start.8) | collective-permute-done | bytes 393248 | tf_op jit(solution)/shard_map/ppermute | solution.py:15
  294.8 2.5 pad_maximum_fusion
  300.0 219.1 %reduce-scatter.2.cloned.1.call-done = bf16[96,768]{1,0:T(8,128)(2,1)} async-done(((bf16[3072,768]{1,0:T(8,128)(2,1)}), bf16[96,768]{1,0:T(8,128)(2,1)}) %reduce-scatter.2.cloned.1.call-update) | async-done | bytes 147472 | tf_op jit(solution)/shard_map/reduce_scatter | solution.py:215
  519.9 63.7 %all-reduce.2.cloned.1.call-done = bf16[96,768]{1,0:T(8,128)(2,1)} async-done(((bf16[96,768]{1,0:T(8,128)(2,1)}), bf16[96,768]{1,0:T(8,128)(2,1)}) %all-reduce.2.cloned.1.call-update) | async-done | bytes 147472 | tf_op jit(solution)/shard_map/psum | solution.py:216
  (175 shorter events, 65.9 us)
Async XLA Ops:
  7.2 511.9 %reduce-scatter.2.cloned.1.call-start = ((), (), s32[]{:S(2)}) async-start(), calls=%async_computation.1 | async-start | bytes 4866048 | tf_op jit(solution)/shard_map/reduce_scatter | solution.py:215
  7.2 21.6 %copy-start.1 = (bf16[768,768]{1,0:T(8,128)(2,1)S(1)}, bf16[768,768]{1,0:T(8,128)(2,1)}, u32[]{:S(2)}) copy-start(bf16[768,768]{1,0:T(8,128)(2,1)} %param.11) | copy-start | bytes 3538948
  10.5 60.5 %collective-permute-start.7 = (bf16[128,768]{1,0:T(8,128)(2,1)}, bf16[128,768]{1,0:T(8,128)(2,1)}, u32[]{:S(2)}, u32[]{:S(2)}) collective-permute-start(bf16[128,768]{1,0:T(8,128)(2,1)} %convolution_convert_fusion.4), channel_id=1, source_target_pairs={{0,1},{1,2},{2,3},{3,4},{4,5},{5,6},{6,7},{7,8},{8,9},{9,10},{10,1... | collective-permute-start | bytes 589832 | tf_op jit(solution)/shard_map/ppermute | solution.py:15
  14.3 49.9 %collective-permute-start.6 = (bf16[128,768]{1,0:T(8,128)(2,1)}, bf16[128,768]{1,0:T(8,128)(2,1)}, u32[]{:S(2)}, u32[]{:S(2)}) collective-permute-start(bf16[128,768]{1,0:T(8,128)(2,1)} %convolution_convert_fusion.4), channel_id=1, source_target_pairs={{0,2},{1,3},{2,4},{3,5},{4,6},{5,7},{6,8},{7,9},{8,10},{9,11},{10,... | collective-permute-start | bytes 589832 | tf_op jit(solution)/shard_map/ppermute | solution.py:15
  19.5 41.1 %collective-permute-start.5 = (bf16[128,768]{1,0:T(8,128)(2,1)}, bf16[128,768]{1,0:T(8,128)(2,1)}, u32[]{:S(2)}, u32[]{:S(2)}) collective-permute-start(bf16[128,768]{1,0:T(8,128)(2,1)} %convolution_convert_fusion.4), channel_id=1, source_target_pairs={{0,3},{1,4},{2,5},{3,6},{4,7},{5,8},{6,9},{7,10},{8,11},{9,12},{10... | collective-permute-start | bytes 589832 | tf_op jit(solution)/shard_map/ppermute | solution.py:15
  25.4 24.5 %collective-permute-start.4 = (bf16[128,768]{1,0:T(8,128)(2,1)}, bf16[128,768]{1,0:T(8,128)(2,1)}, u32[]{:S(2)}, u32[]{:S(2)}) collective-permute-start(bf16[128,768]{1,0:T(8,128)(2,1)} %convolution_convert_fusion.4), channel_id=1, source_target_pairs={{0,4},{1,5},{2,6},{3,7},{4,8},{5,9},{6,10},{7,11},{8,12},{9,13},{1... | collective-permute-start | bytes 589832 | tf_op jit(solution)/shard_map/ppermute | solution.py:15
  30.7 7.0 %copy-start.10 = (bf16[1,128,768]{2,1,0:T(8,128)(2,1)S(1)}, bf16[1,128,768]{2,1,0:T(8,128)(2,1)}, u32[]{:S(2)}) copy-start(bf16[1,128,768]{2,1,0:T(8,128)(2,1)} %param.9) | copy-start | bytes 589828
  32.4 62.0 %collective-permute-start.3 = (bf16[128,768]{0,1:T(8,128)(2,1)}, bf16[128,768]{0,1:T(8,128)(2,1)}, u32[]{:S(2)}, u32[]{:S(2)}) collective-permute-start(bf16[128,768]{0,1:T(8,128)(2,1)} %bitcast.2), channel_id=1, source_target_pairs={{0,1},{1,2},{2,3},{3,4},{4,5},{5,6},{6,7},{7,8},{8,9},{9,10},{10,1... | collective-permute-start | bytes 589832 | tf_op jit(solution)/shard_map/ppermute | solution.py:15
  50.0 42.0 %collective-permute-start.2 = (bf16[128,768]{0,1:T(8,128)(2,1)}, bf16[128,768]{0,1:T(8,128)(2,1)}, u32[]{:S(2)}, u32[]{:S(2)}) collective-permute-start(bf16[128,768]{0,1:T(8,128)(2,1)} %bitcast.2), channel_id=1, source_target_pairs={{0,2},{1,3},{2,4},{3,5},{4,6},{5,7},{6,8},{7,9},{8,10},{9,11},{10,... | collective-permute-start | bytes 589832 | tf_op jit(solution)/shard_map/ppermute | solution.py:15
  60.6 28.8 %collective-permute-start.1 = (bf16[128,768]{0,1:T(8,128)(2,1)}, bf16[128,768]{0,1:T(8,128)(2,1)}, u32[]{:S(2)}, u32[]{:S(2)}) collective-permute-start(bf16[128,768]{0,1:T(8,128)(2,1)} %bitcast.2), channel_id=1, source_target_pairs={{0,3},{1,4},{2,5},{3,6},{4,7},{5,8},{6,9},{7,10},{8,11},{9,12},{10... | collective-permute-start | bytes 589832 | tf_op jit(solution)/shard_map/ppermute | solution.py:15
  64.2 21.9 %collective-permute-start = (bf16[128,768]{0,1:T(8,128)(2,1)}, bf16[128,768]{0,1:T(8,128)(2,1)}, u32[]{:S(2)}, u32[]{:S(2)}) collective-permute-start(bf16[128,768]{0,1:T(8,128)(2,1)} %bitcast.2), channel_id=1, source_target_pairs={{0,4},{1,5},{2,6},{3,7},{4,8},{5,9},{6,10},{7,11},{8,12},{9,13},{1... | collective-permute-start | bytes 589832 | tf_op jit(solution)/shard_map/ppermute | solution.py:15
  76.5 14.0 %copy-start.4 = (bf16[640,768]{0,1:T(8,128)(2,1)S(1)}, bf16[640,768]{0,1:T(8,128)(2,1)}, u32[]{:S(2)}) copy-start(bf16[640,768]{0,1:T(8,128)(2,1)} %copy.23) | copy-start | bytes 2949124
  92.9 4.4 copy-start.23
  137.9 5.2 copy-start.26
  137.9 5.2 copy-start.30
  137.9 5.2 copy-start.42
  152.8 14.2 %copy-start.31 = (bf16[128,4,64]{0,2,1:T(8,128)(2,1)S(1)}, bf16[128,4,64]{0,2,1:T(8,128)(2,1)}, u32[]{:S(2)}) copy-start(bf16[128,4,64]{0,2,1:T(8,128)(2,1)} %fusion.60) | copy-start | bytes 196612
  152.8 14.2 %copy-start.32 = (bf16[128,4,64]{0,2,1:T(8,128)(2,1)S(1)}, bf16[128,4,64]{0,2,1:T(8,128)(2,1)}, u32[]{:S(2)}) copy-start(bf16[128,4,64]{0,2,1:T(8,128)(2,1)} %fusion.59) | copy-start | bytes 196612
  152.8 14.2 %copy-start.21 = (f32[128,4,64]{0,2,1:T(8,128)S(1)}, f32[128,4,64]{0,2,1:T(8,128)}, u32[]{:S(2)}) copy-start(f32[128,4,64]{0,2,1:T(8,128)} %fusion.55) | copy-start | bytes 393220
  152.8 14.2 %copy-start.22 = (f32[128,4,64]{0,2,1:T(8,128)S(1)}, f32[128,4,64]{0,2,1:T(8,128)}, u32[]{:S(2)}) copy-start(f32[128,4,64]{0,2,1:T(8,128)} %fusion.52) | copy-start | bytes 393220
  153.0 14.0 %copy-start.11 = (bf16[1,128,768]{2,1,0:T(8,128)(2,1)S(1)}, bf16[1,128,768]{2,1,0:T(8,128)(2,1)}, u32[]{:S(2)}) copy-start(bf16[1,128,768]{2,1,0:T(8,128)(2,1)} %param.9) | copy-start | bytes 589828
  153.1 24.8 %collective-permute-start.15 = (f32[128,768]{0,1:T(8,128)S(1)}, f32[128,768]{0,1:T(8,128)S(1)}, u32[]{:S(2)}, u32[]{:S(2)}) collective-permute-start(f32[128,768]{0,1:T(8,128)S(1)} %bitcast.119), channel_id=1, source_target_pairs={{4,0},{5,1},{6,2},{7,3},{8,4},{9,5},{10,6},{11,7},{12,8},{13,9},{1... | collective-permute-start | bytes 1179656 | tf_op jit(solution)/shard_map/ppermute | solution.py:15
  156.7 41.5 %collective-permute-start.13 = (f32[128,768]{0,1:T(8,128)S(1)}, f32[128,768]{0,1:T(8,128)S(1)}, u32[]{:S(2)}, u32[]{:S(2)}) collective-permute-start(f32[128,768]{0,1:T(8,128)S(1)} %bitcast.118), channel_id=1, source_target_pairs={{2,0},{3,1},{4,2},{5,3},{6,4},{7,5},{8,6},{9,7},{10,8},{11,9},{12,... | collective-permute-start | bytes 1179656 | tf_op jit(solution)/shard_map/ppermute | solution.py:15
  161.2 56.9 %collective-permute-start.14 = (f32[128,768]{0,1:T(8,128)S(1)}, f32[128,768]{0,1:T(8,128)S(1)}, u32[]{:S(2)}, u32[]{:S(2)}) collective-permute-start(f32[128,768]{0,1:T(8,128)S(1)} %bitcast.117), channel_id=1, source_target_pairs={{3,0},{4,1},{5,2},{6,3},{7,4},{8,5},{9,6},{10,7},{11,8},{12,9},{13... | collective-permute-start | bytes 1179656 | tf_op jit(solution)/shard_map/ppermute | solution.py:15
  163.1 85.5 %collective-permute-start.12 = (f32[128,768]{0,1:T(8,128)S(1)}, f32[128,768]{0,1:T(8,128)S(1)}, u32[]{:S(2)}, u32[]{:S(2)}) collective-permute-start(f32[128,768]{0,1:T(8,128)S(1)} %bitcast.116), channel_id=1, source_target_pairs={{1,0},{2,1},{3,2},{4,3},{5,4},{6,5},{7,6},{8,7},{9,8},{10,9},{11,1... | collective-permute-start | bytes 1179656 | tf_op jit(solution)/shard_map/ppermute | solution.py:15
  165.1 84.2 %collective-permute-start.11 = (f32[128,768]{0,1:T(8,128)S(1)}, f32[128,768]{0,1:T(8,128)S(1)}, u32[]{:S(2)}, u32[]{:S(2)}) collective-permute-start(f32[128,768]{0,1:T(8,128)S(1)} %bitcast.115), channel_id=1, source_target_pairs={{4,0},{5,1},{6,2},{7,3},{8,4},{9,5},{10,6},{11,7},{12,8},{13,9},{1... | collective-permute-start | bytes 1179656 | tf_op jit(solution)/shard_map/ppermute | solution.py:15
  177.9 88.5 %collective-permute-start.9 = (f32[128,768]{0,1:T(8,128)S(1)}, f32[128,768]{0,1:T(8,128)S(1)}, u32[]{:S(2)}, u32[]{:S(2)}) collective-permute-start(f32[128,768]{0,1:T(8,128)S(1)} %bitcast.114), channel_id=1, source_target_pairs={{2,0},{3,1},{4,2},{5,3},{6,4},{7,5},{8,6},{9,7},{10,8},{11,9},{12,... | collective-permute-start | bytes 1179656 | tf_op jit(solution)/shard_map/ppermute | solution.py:15
  198.1 87.0 %collective-permute-start.10 = (f32[128,768]{0,1:T(8,128)S(1)}, f32[128,768]{0,1:T(8,128)S(1)}, u32[]{:S(2)}, u32[]{:S(2)}) collective-permute-start(f32[128,768]{0,1:T(8,128)S(1)} %bitcast.113), channel_id=1, source_target_pairs={{3,0},{4,1},{5,2},{6,3},{7,4},{8,5},{9,6},{10,7},{11,8},{12,9},{13... | collective-permute-start | bytes 1179656 | tf_op jit(solution)/shard_map/ppermute | solution.py:15
  218.1 75.3 %collective-permute-start.8 = (f32[128,768]{0,1:T(8,128)S(1)}, f32[128,768]{0,1:T(8,128)S(1)}, u32[]{:S(2)}, u32[]{:S(2)}) collective-permute-start(f32[128,768]{0,1:T(8,128)S(1)} %bitcast.112), channel_id=1, source_target_pairs={{1,0},{2,1},{3,2},{4,3},{5,4},{6,5},{7,6},{8,7},{9,8},{10,9},{11,1... | collective-permute-start | bytes 1179656 | tf_op jit(solution)/shard_map/ppermute | solution.py:15
  249.2 44.4 %copy-start.18 = (f32[128,32]{0,1:T(8,128)S(1)}, f32[128,32]{0,1:T(8,128)}, u32[]{:S(2)}) copy-start(f32[128,32]{0,1:T(8,128)} %copy-done.17) | copy-start | bytes 49156
  249.2 44.4 %copy-start.20 = (f32[128,32]{0,1:T(8,128)S(1)}, f32[128,32]{0,1:T(8,128)}, u32[]{:S(2)}) copy-start(f32[128,32]{0,1:T(8,128)} %copy-done.19) | copy-start | bytes 49156
  297.3 286.2 %all-reduce.2.cloned.1.call-start = ((), (), s32[]{:S(2)}) async-start(), calls=%async_computation.2 | async-start | bytes 294912 | tf_op jit(solution)/shard_map/psum | solution.py:216
  (34 other events, 63.1 us)
Sparse Core Ops, SparseCore 0:
  297.5 221.5 reduce-scatter.1
  521.4 62.1 all-reduce.1
where the time goes:
time: 593 us; the launch traced here: 592 us
  waiting for transfers between devices  404 us (68%)
  starting transfers between devices  71.6 us (12%)
  matrix products  63.4 us (11%)
  local copies, waits for them, and re-layouts  26.3 us (4%)
  between operations  14.9 us (3%)
  other arithmetic  11.7 us (2%)
    reduce_scatter x1, waiting for transfers between devices, on_device(): lax.psum_scatter(term.astype(jnp.bfloat16), 'seq', scatter_dimension=0, t...  219 us
    ppermute x16, waiting for transfers between devices, shifted(): return lax.ppermute(block, axis, route)  121 us
    ppermute x16, starting transfers between devices, shifted(): return lax.ppermute(block, axis, route)  71.5 us
    psum x1, waiting for transfers between devices, on_device(): weight_grads = lax.psum(shares, 'dp').astype(jnp.float32)  63.7 us
    unnamed x104, local copies, waits for them, and re-layouts  18.4 us
    dot_general x3, matrix products, head_group(): jnp.einsum('hqk,qhd->khd', grad_scores, query_heads, preferred_element_ty...  18.1 us
    dot_general x3, matrix products, head_group(): jnp.einsum('hqk,khd->qhd', grad_scores, key_heads, preferred_element_type...  17 us
  transfers between devices with their start and end apart: 18, of which 11 were waited for; matrix products, arithmetic and copies ran while one was open for 5% of the time, Pallas kernels for 0%

commit v1 on v0

--- a/solution.py
+++ b/solution.py
@@ -213,7 +213,7 @@
         axis=0,
     )
     shares = lax.psum_scatter(term.astype(jnp.bfloat16), "seq", scatter_dimension=0, tiled=True)
-    weight_grads = lax.psum(shares, "dp").astype(jnp.float32)
+    weight_grads = jnp.sum(lax.all_gather(shares, "dp"), axis=0).astype(jnp.float32)
     return (grad_input[None], weight_grads)
 
 

time: 593 us -> 558 us (0.941)
  waiting for transfers between devices: 404 us -> 367 us
    psum x1 -> x0, waiting for transfers between devices: 63.7 us -> none  [on_device(): weight_grads = lax.psum(shares, 'dp').astype(jnp.float32)]
    all_gather x0 -> x1, waiting for transfers between devices: none -> 23.9 us  [on_device(): lax.all_gather(shares, 'dp')]
  transfers between devices with their start and end apart: 18 -> 18, of which waited for: 11 -> 11; matrix products, arithmetic and copies ran while one was open for 5% -> 6% of each run, Pallas kernels for 0% -> 0%
where the time goes in v1:
time: 558 us; the launch traced here: 555 us
  waiting for transfers between devices  367 us (66%)
  starting transfers between devices  71.6 us (13%)
  matrix products  63.4 us (11%)
  local copies, waits for them, and re-layouts  26.3 us (5%)
  between operations  14.9 us (3%)
  other arithmetic  12.2 us (2%)
    reduce_scatter x1, waiting for transfers between devices, on_device(): lax.psum_scatter(term.astype(jnp.bfloat16), 'seq', scatter_dimension=0, t...  222 us
    ppermute x16, waiting for transfers between devices, shifted(): return lax.ppermute(block, axis, route)  121 us
    ppermute x16, starting transfers between devices, shifted(): return lax.ppermute(block, axis, route)  71.5 us
    all_gather x1, waiting for transfers between devices, on_device(): lax.all_gather(shares, 'dp')  23.9 us
    unnamed x104, local copies, waits for them, and re-layouts  18.4 us
    dot_general x3, matrix products, head_group(): jnp.einsum('hqk,qhd->khd', grad_scores, query_heads, preferred_element_ty...  18.1 us
    dot_general x3, matrix products, head_group(): jnp.einsum('hqk,khd->qhd', grad_scores, key_heads, preferred_element_type...  17 us
  transfers between devices with their start and end apart: 18, of which 11 were waited for; matrix products, arithmetic and copies ran while one was open for 6% of the time, Pallas kernels for 0%

profile of v1, /device:TPU:2, one launch (start us, length us, event | category | flops | bytes accessed | tf_op | source)
XLA Modules:
  0.0 555.4 jit_solution(18248105114631787160)
XLA Ops:
  10.5 3.8 collective-permute-start.7
  14.3 5.2 collective-permute-start.6
  19.5 5.9 %collective-permute-start.5 = (bf16[128,768]{1,0:T(8,128)(2,1)}, bf16[128,768]{1,0:T(8,128)(2,1)}, u32[]{:S(2)}, u32[]{:S(2)}) collective-permute-start(bf16[128,768]{1,0:T(8,128)(2,1)} %convolution_convert_fusion.4), channel_id=1, source_target_pairs={{0,3},{1,4},{2,5},{3,6},{4,7},{5,8},{6,9},{7,10},{8,11},{9,12},{10... | collective-permute-start | bytes 589832 | tf_op jit(solution)/shard_map/ppermute | solution.py:15
  25.4 3.4 collective-permute-start.4
  32.4 3.8 collective-permute-start.3
  37.7 2.5 convolution_convert_fusion.5
  44.0 6.0 %collective-permute-done.4 = bf16[128,768]{1,0:T(8,128)(2,1)} collective-permute-done((bf16[128,768]{1,0:T(8,128)(2,1)}, bf16[128,768]{1,0:T(8,128)(2,1)}, u32[]{:S(2)}, u32[]{:S(2)}) %collective-permute-start.4) | collective-permute-done | bytes 196640 | tf_op jit(solution)/shard_map/ppermute | solution.py:15
  50.0 9.0 %collective-permute-start.2 = (bf16[128,768]{0,1:T(8,128)(2,1)}, bf16[128,768]{0,1:T(8,128)(2,1)}, u32[]{:S(2)}, u32[]{:S(2)}) collective-permute-start(bf16[128,768]{0,1:T(8,128)(2,1)} %bitcast.2), channel_id=1, source_target_pairs={{0,2},{1,3},{2,4},{3,5},{4,6},{5,7},{6,8},{7,9},{8,10},{9,11},{10,... | collective-permute-start | bytes 589832 | tf_op jit(solution)/shard_map/ppermute | solution.py:15
  64.2 5.2 collective-permute-start
  76.5 9.6 %collective-permute-done = bf16[128,768]{0,1:T(8,128)(2,1)} collective-permute-done((bf16[128,768]{0,1:T(8,128)(2,1)}, bf16[128,768]{0,1:T(8,128)(2,1)}, u32[]{:S(2)}, u32[]{:S(2)}) %collective-permute-start) | collective-permute-done | bytes 196640 | tf_op jit(solution)/shard_map/ppermute | solution.py:15
  100.7 6.0 %fusion.55 = f32[128,4,64]{0,2,1:T(8,128)} fusion(bf16[640,12,64]{0,2,1:T(8,128)(2,1)} %bitcast.123, f32[4,128,640]{2,1,0:T(8,128)} %fusion.68, f32[4,128,640]{2,1,0:T(8,128)} %copy-done.8, f32[4,128]{1,0:T(4,128)} %copy-done.43), kind=kOutput, calls=%fused_computation.66 | convolution fusion | flops 44237952 | bytes 3737600 | tf_op jit(solution)/shard_map/hqk,khd->qhd/dot_general | solution.py:109
  106.7 6.1 %convolution_bitcast_fusion.3 = f32[640,4,64]{0,2,1:T(8,128)} fusion(f32[4,128,640]{2,1,0:T(8,128)} %fusion.68, bf16[128,12,32]{0,2,1:T(8,128)(2,1)} %get-tuple-element.17, bf16[128,12,32]{0,2,1:T(8,128)(2,1)} %get-tuple-element.16, f32[4,128,640]{2,1,0:T(8,128)} %copy-done.8, f32[4,128]{1,0:T(4,128)} %copy-done.43), kind=kOutput, calls=%fused_computation.46 | convolution fusion | flops 44631168 | bytes 3475456 | tf_op jit(solution)/shard_map/hqk,qhd->khd/dot_general | solution.py:112
  112.8 2.6 convolution_bitcast_fusion
  119.8 5.8 %fusion.52 = f32[128,4,64]{0,2,1:T(8,128)} fusion(bf16[640,12,64]{0,2,1:T(8,128)(2,1)} %bitcast.125, f32[4,128,640]{2,1,0:T(8,128)} %fusion.71, f32[4,128,640]{2,1,0:T(8,128)} %copy-done.9, f32[4,128]{1,0:T(4,128)} %copy-done.44), kind=kOutput, calls=%fused_computation.65 | convolution fusion | flops 44237952 | bytes 3737600 | tf_op jit(solution)/shard_map/hqk,khd->qhd/dot_general | solution.py:109
  125.6 6.0 %convolution_bitcast_fusion.4 = f32[640,4,64]{0,2,1:T(8,128)} fusion(f32[4,128,640]{2,1,0:T(8,128)} %fusion.71, bf16[128,12,32]{0,2,1:T(8,128)(2,1)} %get-tuple-element.17, bf16[128,12,32]{0,2,1:T(8,128)(2,1)} %get-tuple-element.16, f32[4,128,640]{2,1,0:T(8,128)} %copy-done.9, f32[4,128]{1,0:T(4,128)} %copy-done.44), kind=kOutput, calls=%fused_computation.47 | convolution fusion | flops 44631168 | bytes 3475456 | tf_op jit(solution)/shard_map/hqk,qhd->khd/dot_general | solution.py:112
  131.6 2.6 convolution_bitcast_fusion.1
  138.0 5.2 fusion.49
  143.2 5.9 %convolution_bitcast_fusion.5 = f32[640,4,64]{0,2,1:T(8,128)} fusion(f32[4,128,640]{2,1,0:T(8,128)} %fusion.74, bf16[128,12,32]{0,2,1:T(8,128)(2,1)S(1)} %copy-done.30, bf16[128,12,32]{0,2,1:T(8,128)(2,1)S(1)} %copy-done.26, f32[4,128,640]{2,1,0:T(8,128)} %copy-done.7, f32[4,128]{1,0:T(4,128)S(1)} %copy-done.42), kind=kOutput, calls=%fused_computation.48 | convolution fusion | flops 44631168 | bytes 3475456 | tf_op jit(solution)/shard_map/hqk,qhd->khd/dot_general | solution.py:112
  153.1 3.6 collective-permute-start.15
  156.7 4.5 collective-permute-start.13
  167.6 10.3 %collective-permute-done.15 = f32[128,768]{0,1:T(8,128)S(1)} collective-permute-done((f32[128,768]{0,1:T(8,128)S(1)}, f32[128,768]{0,1:T(8,128)S(1)}, u32[]{:S(2)}, u32[]{:S(2)}) %collective-permute-start.15) | collective-permute-done | bytes 393248 | tf_op jit(solution)/shard_map/ppermute | solution.py:15
  177.9 7.2 %collective-permute-start.9 = (f32[128,768]{0,1:T(8,128)S(1)}, f32[128,768]{0,1:T(8,128)S(1)}, u32[]{:S(2)}, u32[]{:S(2)}) collective-permute-start(f32[128,768]{0,1:T(8,128)S(1)} %bitcast.116), channel_id=1, source_target_pairs={{2,0},{3,1},{4,2},{5,3},{6,4},{7,5},{8,6},{9,7},{10,8},{11,9},{12,... | collective-permute-start | bytes 1179656 | tf_op jit(solution)/shard_map/ppermute | solution.py:15
  185.1 13.0 %collective-permute-done.13 = f32[128,768]{0,1:T(8,128)S(1)} collective-permute-done((f32[128,768]{0,1:T(8,128)S(1)}, f32[128,768]{0,1:T(8,128)S(1)}, u32[]{:S(2)}, u32[]{:S(2)}) %collective-permute-start.13) | collective-permute-done | bytes 393248 | tf_op jit(solution)/shard_map/ppermute | solution.py:15
  198.1 10.3 %collective-permute-start.10 = (f32[128,768]{0,1:T(8,128)S(1)}, f32[128,768]{0,1:T(8,128)S(1)}, u32[]{:S(2)}, u32[]{:S(2)}) collective-permute-start(f32[128,768]{0,1:T(8,128)S(1)} %bitcast.115), channel_id=1, source_target_pairs={{3,0},{4,1},{5,2},{6,3},{7,4},{8,5},{9,6},{10,7},{11,8},{12,9},{13... | collective-permute-start | bytes 1179656 | tf_op jit(solution)/shard_map/ppermute | solution.py:15
  208.4 9.7 %collective-permute-done.14 = f32[128,768]{0,1:T(8,128)S(1)} collective-permute-done((f32[128,768]{0,1:T(8,128)S(1)}, f32[128,768]{0,1:T(8,128)S(1)}, u32[]{:S(2)}, u32[]{:S(2)}) %collective-permute-start.14) | collective-permute-done | bytes 393248 | tf_op jit(solution)/shard_map/ppermute | solution.py:15
  220.0 28.5 %collective-permute-done.12 = f32[128,768]{0,1:T(8,128)S(1)} collective-permute-done((f32[128,768]{0,1:T(8,128)S(1)}, f32[128,768]{0,1:T(8,128)S(1)}, u32[]{:S(2)}, u32[]{:S(2)}) %collective-permute-start.12) | collective-permute-done | bytes 393248 | tf_op jit(solution)/shard_map/ppermute | solution.py:15
  249.3 17.1 %collective-permute-done.9 = f32[128,768]{0,1:T(8,128)S(1)} collective-permute-done((f32[128,768]{0,1:T(8,128)S(1)}, f32[128,768]{0,1:T(8,128)S(1)}, u32[]{:S(2)}, u32[]{:S(2)}) %collective-permute-start.9) | collective-permute-done | bytes 393248 | tf_op jit(solution)/shard_map/ppermute | solution.py:15
  266.3 18.8 %collective-permute-done.10 = f32[128,768]{0,1:T(8,128)S(1)} collective-permute-done((f32[128,768]{0,1:T(8,128)S(1)}, f32[128,768]{0,1:T(8,128)S(1)}, u32[]{:S(2)}, u32[]{:S(2)}) %collective-permute-start.10) | collective-permute-done | bytes 393248 | tf_op jit(solution)/shard_map/ppermute | solution.py:15
  285.1 8.3 %collective-permute-done.8 = f32[128,768]{0,1:T(8,128)S(1)} collective-permute-done((f32[128,768]{0,1:T(8,128)S(1)}, f32[128,768]{0,1:T(8,128)S(1)}, u32[]{:S(2)}, u32[]{:S(2)}) %collective-permute-start.8) | collective-permute-done | bytes 393248 | tf_op jit(solution)/shard_map/ppermute | solution.py:15
  294.8 2.5 pad_maximum_fusion
  297.4 221.7 %reduce-scatter.2.cloned.1.call-done = bf16[96,768]{1,0:T(8,128)(2,1)} async-done(((bf16[3072,768]{1,0:T(8,128)(2,1)}), bf16[96,768]{1,0:T(8,128)(2,1)}) %reduce-scatter.2.cloned.1.call-update) | async-done | bytes 147472 | tf_op jit(solution)/shard_map/reduce_scatter | solution.py:215
  522.5 23.9 %all-gather.3.cloned.1.call-done = bf16[768,768]{1,0:T(8,128)(2,1)} async-done(((bf16[96,768]{1,0:T(8,128)(2,1)}), bf16[768,768]{1,0:T(8,128)(2,1)}) %all-gather.3.cloned.1.call-update) | async-done | bytes 1179664 | tf_op jit(solution)/shard_map/all_gather | solution.py:216
  (176 shorter events, 66.4 us)
Async XLA Ops:
  7.2 511.9 %reduce-scatter.2.cloned.1.call-start = ((), (), s32[]{:S(2)}) async-start(), calls=%async_computation.1 | async-start | bytes 4866048 | tf_op jit(solution)/shard_map/reduce_scatter | solution.py:215
  7.2 21.6 %copy-start.1 = (bf16[768,768]{1,0:T(8,128)(2,1)S(1)}, bf16[768,768]{1,0:T(8,128)(2,1)}, u32[]{:S(2)}) copy-start(bf16[768,768]{1,0:T(8,128)(2,1)} %param.11) | copy-start | bytes 3538948
  10.5 60.5 %collective-permute-start.7 = (bf16[128,768]{1,0:T(8,128)(2,1)}, bf16[128,768]{1,0:T(8,128)(2,1)}, u32[]{:S(2)}, u32[]{:S(2)}) collective-permute-start(bf16[128,768]{1,0:T(8,128)(2,1)} %convolution_convert_fusion.4), channel_id=1, source_target_pairs={{0,1},{1,2},{2,3},{3,4},{4,5},{5,6},{6,7},{7,8},{8,9},{9,10},{10,1... | collective-permute-start | bytes 589832 | tf_op jit(solution)/shard_map/ppermute | solution.py:15
  14.3 49.9 %collective-permute-start.6 = (bf16[128,768]{1,0:T(8,128)(2,1)}, bf16[128,768]{1,0:T(8,128)(2,1)}, u32[]{:S(2)}, u32[]{:S(2)}) collective-permute-start(bf16[128,768]{1,0:T(8,128)(2,1)} %convolution_convert_fusion.4), channel_id=1, source_target_pairs={{0,2},{1,3},{2,4},{3,5},{4,6},{5,7},{6,8},{7,9},{8,10},{9,11},{10,... | collective-permute-start | bytes 589832 | tf_op jit(solution)/shard_map/ppermute | solution.py:15
  19.5 41.1 %collective-permute-start.5 = (bf16[128,768]{1,0:T(8,128)(2,1)}, bf16[128,768]{1,0:T(8,128)(2,1)}, u32[]{:S(2)}, u32[]{:S(2)}) collective-permute-start(bf16[128,768]{1,0:T(8,128)(2,1)} %convolution_convert_fusion.4), channel_id=1, source_target_pairs={{0,3},{1,4},{2,5},{3,6},{4,7},{5,8},{6,9},{7,10},{8,11},{9,12},{10... | collective-permute-start | bytes 589832 | tf_op jit(solution)/shard_map/ppermute | solution.py:15
  25.4 24.5 %collective-permute-start.4 = (bf16[128,768]{1,0:T(8,128)(2,1)}, bf16[128,768]{1,0:T(8,128)(2,1)}, u32[]{:S(2)}, u32[]{:S(2)}) collective-permute-start(bf16[128,768]{1,0:T(8,128)(2,1)} %convolution_convert_fusion.4), channel_id=1, source_target_pairs={{0,4},{1,5},{2,6},{3,7},{4,8},{5,9},{6,10},{7,11},{8,12},{9,13},{1... | collective-permute-start | bytes 589832 | tf_op jit(solution)/shard_map/ppermute | solution.py:15
  30.7 7.0 %copy-start.10 = (bf16[1,128,768]{2,1,0:T(8,128)(2,1)S(1)}, bf16[1,128,768]{2,1,0:T(8,128)(2,1)}, u32[]{:S(2)}) copy-start(bf16[1,128,768]{2,1,0:T(8,128)(2,1)} %param.9) | copy-start | bytes 589828
  32.4 62.0 %collective-permute-start.3 = (bf16[128,768]{0,1:T(8,128)(2,1)}, bf16[128,768]{0,1:T(8,128)(2,1)}, u32[]{:S(2)}, u32[]{:S(2)}) collective-permute-start(bf16[128,768]{0,1:T(8,128)(2,1)} %bitcast.2), channel_id=1, source_target_pairs={{0,1},{1,2},{2,3},{3,4},{4,5},{5,6},{6,7},{7,8},{8,9},{9,10},{10,1... | collective-permute-start | bytes 589832 | tf_op jit(solution)/shard_map/ppermute | solution.py:15
  50.0 42.0 %collective-permute-start.2 = (bf16[128,768]{0,1:T(8,128)(2,1)}, bf16[128,768]{0,1:T(8,128)(2,1)}, u32[]{:S(2)}, u32[]{:S(2)}) collective-permute-start(bf16[128,768]{0,1:T(8,128)(2,1)} %bitcast.2), channel_id=1, source_target_pairs={{0,2},{1,3},{2,4},{3,5},{4,6},{5,7},{6,8},{7,9},{8,10},{9,11},{10,... | collective-permute-start | bytes 589832 | tf_op jit(solution)/shard_map/ppermute | solution.py:15
  60.6 28.8 %collective-permute-start.1 = (bf16[128,768]{0,1:T(8,128)(2,1)}, bf16[128,768]{0,1:T(8,128)(2,1)}, u32[]{:S(2)}, u32[]{:S(2)}) collective-permute-start(bf16[128,768]{0,1:T(8,128)(2,1)} %bitcast.2), channel_id=1, source_target_pairs={{0,3},{1,4},{2,5},{3,6},{4,7},{5,8},{6,9},{7,10},{8,11},{9,12},{10... | collective-permute-start | bytes 589832 | tf_op jit(solution)/shard_map/ppermute | solution.py:15
  64.2 21.9 %collective-permute-start = (bf16[128,768]{0,1:T(8,128)(2,1)}, bf16[128,768]{0,1:T(8,128)(2,1)}, u32[]{:S(2)}, u32[]{:S(2)}) collective-permute-start(bf16[128,768]{0,1:T(8,128)(2,1)} %bitcast.2), channel_id=1, source_target_pairs={{0,4},{1,5},{2,6},{3,7},{4,8},{5,9},{6,10},{7,11},{8,12},{9,13},{1... | collective-permute-start | bytes 589832 | tf_op jit(solution)/shard_map/ppermute | solution.py:15
  76.5 14.0 %copy-start.4 = (bf16[640,768]{0,1:T(8,128)(2,1)S(1)}, bf16[640,768]{0,1:T(8,128)(2,1)}, u32[]{:S(2)}) copy-start(bf16[640,768]{0,1:T(8,128)(2,1)} %copy.23) | copy-start | bytes 2949124
  92.9 4.4 copy-start.23
  137.9 5.2 copy-start.26
  137.9 5.2 copy-start.30
  137.9 5.2 copy-start.42
  152.8 14.2 %copy-start.31 = (bf16[128,4,64]{0,2,1:T(8,128)(2,1)S(1)}, bf16[128,4,64]{0,2,1:T(8,128)(2,1)}, u32[]{:S(2)}) copy-start(bf16[128,4,64]{0,2,1:T(8,128)(2,1)} %fusion.60) | copy-start | bytes 196612
  152.8 14.2 %copy-start.32 = (bf16[128,4,64]{0,2,1:T(8,128)(2,1)S(1)}, bf16[128,4,64]{0,2,1:T(8,128)(2,1)}, u32[]{:S(2)}) copy-start(bf16[128,4,64]{0,2,1:T(8,128)(2,1)} %fusion.59) | copy-start | bytes 196612
  152.8 14.2 %copy-start.21 = (f32[128,4,64]{0,2,1:T(8,128)S(1)}, f32[128,4,64]{0,2,1:T(8,128)}, u32[]{:S(2)}) copy-start(f32[128,4,64]{0,2,1:T(8,128)} %fusion.55) | copy-start | bytes 393220
  152.8 14.2 %copy-start.22 = (f32[128,4,64]{0,2,1:T(8,128)S(1)}, f32[128,4,64]{0,2,1:T(8,128)}, u32[]{:S(2)}) copy-start(f32[128,4,64]{0,2,1:T(8,128)} %fusion.52) | copy-start | bytes 393220
  153.0 14.0 %copy-start.11 = (bf16[1,128,768]{2,1,0:T(8,128)(2,1)S(1)}, bf16[1,128,768]{2,1,0:T(8,128)(2,1)}, u32[]{:S(2)}) copy-start(bf16[1,128,768]{2,1,0:T(8,128)(2,1)} %param.9) | copy-start | bytes 589828
  153.1 24.8 %collective-permute-start.15 = (f32[128,768]{0,1:T(8,128)S(1)}, f32[128,768]{0,1:T(8,128)S(1)}, u32[]{:S(2)}, u32[]{:S(2)}) collective-permute-start(f32[128,768]{0,1:T(8,128)S(1)} %bitcast.121), channel_id=1, source_target_pairs={{4,0},{5,1},{6,2},{7,3},{8,4},{9,5},{10,6},{11,7},{12,8},{13,9},{1... | collective-permute-start | bytes 1179656 | tf_op jit(solution)/shard_map/ppermute | solution.py:15
  156.7 41.5 %collective-permute-start.13 = (f32[128,768]{0,1:T(8,128)S(1)}, f32[128,768]{0,1:T(8,128)S(1)}, u32[]{:S(2)}, u32[]{:S(2)}) collective-permute-start(f32[128,768]{0,1:T(8,128)S(1)} %bitcast.120), channel_id=1, source_target_pairs={{2,0},{3,1},{4,2},{5,3},{6,4},{7,5},{8,6},{9,7},{10,8},{11,9},{12,... | collective-permute-start | bytes 1179656 | tf_op jit(solution)/shard_map/ppermute | solution.py:15
  161.2 56.9 %collective-permute-start.14 = (f32[128,768]{0,1:T(8,128)S(1)}, f32[128,768]{0,1:T(8,128)S(1)}, u32[]{:S(2)}, u32[]{:S(2)}) collective-permute-start(f32[128,768]{0,1:T(8,128)S(1)} %bitcast.119), channel_id=1, source_target_pairs={{3,0},{4,1},{5,2},{6,3},{7,4},{8,5},{9,6},{10,7},{11,8},{12,9},{13... | collective-permute-start | bytes 1179656 | tf_op jit(solution)/shard_map/ppermute | solution.py:15
  163.1 85.5 %collective-permute-start.12 = (f32[128,768]{0,1:T(8,128)S(1)}, f32[128,768]{0,1:T(8,128)S(1)}, u32[]{:S(2)}, u32[]{:S(2)}) collective-permute-start(f32[128,768]{0,1:T(8,128)S(1)} %bitcast.118), channel_id=1, source_target_pairs={{1,0},{2,1},{3,2},{4,3},{5,4},{6,5},{7,6},{8,7},{9,8},{10,9},{11,1... | collective-permute-start | bytes 1179656 | tf_op jit(solution)/shard_map/ppermute | solution.py:15
  165.1 84.2 %collective-permute-start.11 = (f32[128,768]{0,1:T(8,128)S(1)}, f32[128,768]{0,1:T(8,128)S(1)}, u32[]{:S(2)}, u32[]{:S(2)}) collective-permute-start(f32[128,768]{0,1:T(8,128)S(1)} %bitcast.117), channel_id=1, source_target_pairs={{4,0},{5,1},{6,2},{7,3},{8,4},{9,5},{10,6},{11,7},{12,8},{13,9},{1... | collective-permute-start | bytes 1179656 | tf_op jit(solution)/shard_map/ppermute | solution.py:15
  177.9 88.5 %collective-permute-start.9 = (f32[128,768]{0,1:T(8,128)S(1)}, f32[128,768]{0,1:T(8,128)S(1)}, u32[]{:S(2)}, u32[]{:S(2)}) collective-permute-start(f32[128,768]{0,1:T(8,128)S(1)} %bitcast.116), channel_id=1, source_target_pairs={{2,0},{3,1},{4,2},{5,3},{6,4},{7,5},{8,6},{9,7},{10,8},{11,9},{12,... | collective-permute-start | bytes 1179656 | tf_op jit(solution)/shard_map/ppermute | solution.py:15
  198.1 87.0 %collective-permute-start.10 = (f32[128,768]{0,1:T(8,128)S(1)}, f32[128,768]{0,1:T(8,128)S(1)}, u32[]{:S(2)}, u32[]{:S(2)}) collective-permute-start(f32[128,768]{0,1:T(8,128)S(1)} %bitcast.115), channel_id=1, source_target_pairs={{3,0},{4,1},{5,2},{6,3},{7,4},{8,5},{9,6},{10,7},{11,8},{12,9},{13... | collective-permute-start | bytes 1179656 | tf_op jit(solution)/shard_map/ppermute | solution.py:15
  218.1 75.3 %collective-permute-start.8 = (f32[128,768]{0,1:T(8,128)S(1)}, f32[128,768]{0,1:T(8,128)S(1)}, u32[]{:S(2)}, u32[]{:S(2)}) collective-permute-start(f32[128,768]{0,1:T(8,128)S(1)} %bitcast.114), channel_id=1, source_target_pairs={{1,0},{2,1},{3,2},{4,3},{5,4},{6,5},{7,6},{8,7},{9,8},{10,9},{11,1... | collective-permute-start | bytes 1179656 | tf_op jit(solution)/shard_map/ppermute | solution.py:15
  249.2 44.4 %copy-start.18 = (f32[128,32]{0,1:T(8,128)S(1)}, f32[128,32]{0,1:T(8,128)}, u32[]{:S(2)}) copy-start(f32[128,32]{0,1:T(8,128)} %copy-done.17) | copy-start | bytes 49156
  249.2 44.4 %copy-start.20 = (f32[128,32]{0,1:T(8,128)S(1)}, f32[128,32]{0,1:T(8,128)}, u32[]{:S(2)}) copy-start(f32[128,32]{0,1:T(8,128)} %copy-done.19) | copy-start | bytes 49156
  297.3 249.0 %all-gather.3.cloned.1.call-start = ((), (), s32[]{:S(2)}) async-start(), calls=%async_computation.2 | async-start | bytes 1327104 | tf_op jit(solution)/shard_map/all_gather | solution.py:216
  (34 other events, 63.1 us)
Sparse Core Ops, SparseCore 0:
  297.5 221.5 reduce-scatter.1
  520.9 25.4 all-gather.2
